TPU v7x, 32 devices: a whole 2x2x4 slice. The times are simulated.
32 devices in a mesh: chan: 2 (over x), srow: 4 (over y, core), scol: 4 (over z).
Axes of the slice: x: 2, y: 2, z: 4, core: 2. Of those that a mesh axis runs over, the one named last changes fastest.
Arguments:
- vis: bfloat16 [2, 2, 512, 512], P('chan', None, 'srow', 'scol'), may hold values from -4 to 4
- model: bfloat16 [2, 64, 2, 512, 512], P('chan', None, None, 'srow', 'scol'), may hold values from -1 to 1, as said below
- flags: int32 [2, 32, 32], P('chan', 'srow', 'scol'), may hold values 0 or 1
- gains: float32 [2, 64, 2, 512], P('chan', None, None, ('srow', 'scol')), may hold values from -3 to 3
- consensus: float32 [64, 1, 2, 512], P(None, None, None, ('srow', 'scol')), may hold values from -3 to 3
- dual: float32 [2, 64, 2, 512], P('chan', None, None, ('srow', 'scol')), may hold values from -2 to 2
- rho: float32 [8], replicated, may hold values from 0.5 to 8
- cluster: int32 [64], replicated, may hold values from 0 to 7
Outputs:
- gains_out: float32 [2, 64, 2, 512], P('chan', None, None, ('srow', 'scol'))
- consensus_out: float32 [64, 1, 2, 512], P(None, None, None, ('srow', 'scol'))
- dual_out: float32 [2, 64, 2, 512], P('chan', None, None, ('srow', 'scol'))
Inputs may be any that keep to these rules, and one draw needn't show every extreme that they name: `model`: entries of about 1 / sqrt(512) in size.
All inputs are finite; a program needn't handle non-finite values. No bound on the sum of `flags` on one device may be relied on, other than what follows from the above.
Results may differ from a plain program's by a relative error of at most 0.0003.
Values sent between devices are 32-bit elements; how exact they have to be, the bound alone decides.
No kernel may reach another device: no remote copies, remote signals or barrier semaphores. Data moves between devices by JAX's collectives and lax.ppermute only.
A program may use at most 64 MiB of HBM per device.

v0:
```python
import math
import jax
import jax.numpy as jnp
from jax import lax
from jax.sharding import PartitionSpec as P

STATIONS = 512
TILE = 16
ITERS = 4
EPS = 1e-05
STEP = 0.5


def basis_table(groups, order):
    xval = (jnp.arange(groups, dtype=jnp.float32) + 0.5) / groups
    columns = [
        math.comb(order - 1, b) * xval**b * (1.0 - xval) ** (order - 1 - b) for b in range(order)
    ]
    return jnp.stack(columns, axis=1)


def local_terms(vis_block, model_block, weight, g_row, g_col):
    m_real = model_block[:, 0].astype(jnp.float32)
    m_imag = model_block[:, 1].astype(jnp.float32)
    c_real = g_col[:, 0][:, None, :]
    c_imag = g_col[:, 1][:, None, :]
    z_real = m_real * c_real + m_imag * c_imag
    z_imag = m_imag * c_real - m_real * c_imag
    r_real = g_row[:, 0][:, :, None]
    r_imag = g_row[:, 1][:, :, None]
    pred_real = jnp.sum(r_real * z_real - r_imag * z_imag, axis=0)
    pred_imag = jnp.sum(r_real * z_imag + r_imag * z_real, axis=0)
    res_real = vis_block[0].astype(jnp.float32) - pred_real
    res_imag = vis_block[1].astype(jnp.float32) - pred_imag
    w_real = weight * res_real
    w_imag = weight * res_imag
    power = jnp.sum(w_real * res_real + w_imag * res_imag)
    a_term = jnp.sum(weight[None] * (z_real * z_real + z_imag * z_imag), axis=-1)
    cross_real = jnp.sum(z_real * w_real[None] + z_imag * w_imag[None], axis=-1)
    cross_imag = jnp.sum(z_real * w_imag[None] - z_imag * w_real[None], axis=-1)
    return (power, a_term, jnp.stack([cross_real, cross_imag], axis=-2))


def solve(cross, a_term, g_now, target, rho_eff):
    denom = a_term + rho_eff[:, None]
    fresh = (cross + a_term[..., None, :] * g_now + rho_eff[:, None, None] * target) / denom[
        ..., None, :
    ]
    return g_now + STEP * (fresh - g_now)


def gram_solve(table, rhs):
    gram = jnp.dot(table.T, table, precision=lax.Precision.HIGHEST)
    factor = jnp.linalg.cholesky(gram)
    order = rhs.shape[1]
    flat = jnp.moveaxis(rhs, 1, 0).reshape(order, -1)
    sol = jax.scipy.linalg.cho_solve((factor, True), flat)
    return jnp.moveaxis(sol.reshape((order, rhs.shape[0]) + rhs.shape[2:]), 0, 1)


def sweep_terms(vis_block, model_block, weight, g_row, own_gains, rho_dir, groups):
    g_col = lax.all_gather(own_gains, "srow", axis=2, tiled=True)
    power, a_term, cross = local_terms(vis_block, model_block, weight, g_row, g_col)
    total = lax.psum(power, ("chan", "srow", "scol"))
    rho_eff = rho_dir * (total / (groups * STATIONS * STATIONS) + EPS)
    return (a_term, cross, rho_eff)


def shards(vis, model, flags, gains, consensus, dual, rho, cluster):
    groups = lax.axis_size("chan")
    order = consensus.shape[1]
    table = basis_table(groups, order)
    brow = lax.dynamic_index_in_dim(table, lax.axis_index("chan"), 0, keepdims=False)
    matches = cluster[:, None] == jnp.arange(rho.shape[0], dtype=jnp.int32)[None, :]
    rho_dir = jnp.sum(jnp.where(matches, rho[None, :], 0.0), axis=1)
    fl = flags[0].astype(jnp.float32)
    weight = jnp.repeat(jnp.repeat(fl, TILE, axis=0), TILE, axis=1)
    vis_block = vis[0]
    model_block = model[0]
    dual_own = dual[0]
    target = jnp.einsum("b,kbcp->kcp", brow, consensus, precision=lax.Precision.HIGHEST) - dual_own
    g = gains[0]
    for step in range(ITERS):
        g_row = lax.all_gather(g, "scol", axis=2, tiled=True)
        a_term, cross, rho_eff = sweep_terms(
            vis_block, model_block, weight, g_row, g, rho_dir, groups
        )
        a_own, cross_own = (
            lax.psum_scatter(a_term[:, None, :], "scol", scatter_dimension=2, tiled=True),
            lax.psum_scatter(cross, "scol", scatter_dimension=2, tiled=True),
        )
        g = solve(cross_own, a_own[:, 0, :], g, target, rho_eff)
    local = brow[None, :, None, None] * (g + dual_own)[:, None, :, :]
    sums = lax.psum(local, "chan")
    coeffs = gram_solve(table, sums)
    dual_new = (
        dual_own + g - jnp.einsum("b,kbcp->kcp", brow, coeffs, precision=lax.Precision.HIGHEST)
    )
    return (g[None], coeffs, dual_new[None])


def solution(mesh):
    placed = (
        P("chan", None, "srow", "scol"),
        P("chan", None, None, "srow", "scol"),
        P("chan", "srow", "scol"),
        P("chan", None, None, ("srow", "scol")),
        P(None, None, None, ("srow", "scol")),
        P("chan", None, None, ("srow", "scol")),
        P(),
        P(),
    )
    return jax.shard_map(
        shards,
        mesh=mesh,
        in_specs=placed,
        out_specs=(
            P("chan", None, None, ("srow", "scol")),
            P(None, None, None, ("srow", "scol")),
            P("chan", None, None, ("srow", "scol")),
        ),
        check_vma=False,
    )
```

profile of v0, /device:TPU:0, one launch (start us, length us, event | category | flops | bytes accessed | tf_op | source)
XLA Modules:
  0.0 436.5 jit_solution(12146551925661814514)
XLA Ops:
  7.2 15.3 %all-gather.1 = f32[1,64,2,128]{1,3,2,0:T(8,128)S(1)} all-gather(f32[1,64,2,32]{1,3,2,0:T(8,128)} %param.11), channel_id=3, replica_groups=mesh['chan'=2,'srow'=4,'scol'=4] {'scol'}, dimensions={3}, use_global_device_ids=true | all-gather | bytes 81920 | tf_op jit(solution)/shard_map/all_gather | solution.py:84
  22.5 5.6 %all-gather = f32[1,64,2,128]{1,3,2,0:T(8,128)S(1)} all-gather(f32[1,64,2,32]{1,3,2,0:T(8,128)} %param.11), channel_id=2, replica_groups=mesh['chan'=2,'srow'=4,'scol'=4] {'srow'}, dimensions={3}, use_global_device_ids=true | all-gather | bytes 81920 | tf_op jit(solution)/shard_map/all_gather | solution.py:62
  29.6 6.2 %subtract_reduce_fusion.7 = (f32[128,128]{1,0:T(8,128)S(1)}, f32[128,128]{1,0:T(8,128)S(1)}) fusion(f32[64,128]{1,0:T(8,128)S(1)} %copy.125, f32[64,128]{1,0:T(8,128)S(1)} %copy.124, f32[64,128]{1,0:T(8,128)S(1)} %copy.122, f32[64,128]{1,0:T(8,128)S(1)} %copy.121, bf16[64,2,128,128]{3,2,1,0:T(8,128)(2,1)} %bitcast.195), kind=kLoop, calls=%fused_computation.43 | loop fusion | flops 16744448 | bytes 4456448 | tf_op jit(solution)/shard_map/reduce_sum | solution.py:31
  36.4 4.1 add_reduce_fusion.6
  41.4 0.8 copy.128
  44.0 41.0 %psum.35 = f32[]{:T(128)} all-reduce(f32[]{:T(128)} %get-tuple-element.47), channel_id=1, replica_groups=mesh['chan'=2,'srow'=4,'scol'=4] {'chan','srow','scol'}, use_global_device_ids=true, to_apply=%region_9.10 | all-reduce | flops 1 | bytes 8 | tf_op jit(solution)/shard_map/psum | solution.py:64
  87.9 9.0 %all-reduce.9.cloned.1.call-done = f32[64,2,128]{0,1,2:T(2,128)} async-done(((f32[64,2,128]{0,1,2:T(2,128)}), f32[64,2,128]{0,1,2:T(2,128)}) %all-reduce.9.cloned.1.call-update) | async-done | bytes 65552
  96.9 0.9 bitcast_add_fusion.1
  97.8 13.5 %all_gather.27 = f32[64,2,128]{0,1,2:T(2,128)S(1)} all-gather(f32[64,2,32]{0,1,2:T(2,128)S(1)} %get-tuple-element.45), channel_id=1, replica_groups=mesh['chan'=2,'srow'=4,'scol'=4] {'scol'}, dimensions={2}, use_global_device_ids=true | all-gather | bytes 81920 | tf_op jit(solution)/shard_map/all_gather | solution.py:84
  111.3 5.4 %all_gather.26 = f32[64,2,128]{0,1,2:T(2,128)S(1)} all-gather(f32[64,2,32]{0,1,2:T(2,128)S(1)} %get-tuple-element.45), channel_id=1, replica_groups=mesh['chan'=2,'srow'=4,'scol'=4] {'srow'}, dimensions={2}, use_global_device_ids=true | all-gather | bytes 81920 | tf_op jit(solution)/shard_map/all_gather | solution.py:62
  117.3 6.2 %subtract_reduce_fusion.5 = (f32[128,128]{1,0:T(8,128)S(1)}, f32[128,128]{1,0:T(8,128)S(1)}) fusion(f32[64,128]{1,0:T(8,128)S(1)} %copy.136, f32[64,128]{1,0:T(8,128)S(1)} %copy.135, f32[64,128]{1,0:T(8,128)S(1)} %copy.134, f32[64,128]{1,0:T(8,128)S(1)} %copy.133, bf16[64,2,128,128]{3,2,1,0:T(8,128)(2,1)} %bitcast.196), kind=kLoop, calls=%fused_computation.38 | loop fusion | flops 16744448 | bytes 4456448 | tf_op jit(solution)/shard_map/reduce_sum | solution.py:31
  124.1 4.1 add_reduce_fusion.4
  129.0 39.0 %psum.36 = f32[]{:T(128)} all-reduce(f32[]{:T(128)} %get-tuple-element.42), channel_id=1, replica_groups=mesh['chan'=2,'srow'=4,'scol'=4] {'chan','srow','scol'}, use_global_device_ids=true, to_apply=%region_18.19 | all-reduce | flops 1 | bytes 8 | tf_op jit(solution)/shard_map/psum | solution.py:64
  168.7 0.8 copy.139
  170.3 33.9 %all-reduce.11.cloned.1.call-done = f32[64,2,128]{0,1,2:T(2,128)} async-done(((f32[64,2,128]{0,1,2:T(2,128)}), f32[64,2,128]{0,1,2:T(2,128)}) %all-reduce.11.cloned.1.call-update) | async-done | bytes 65552
  204.2 0.8 multiply_add_fusion.2
  205.0 13.5 %all_gather.29 = f32[64,2,128]{0,1,2:T(2,128)S(1)} all-gather(f32[64,2,32]{0,1,2:T(2,128)S(1)} %multiply_add_fusion.2), channel_id=1, replica_groups=mesh['chan'=2,'srow'=4,'scol'=4] {'scol'}, dimensions={2}, use_global_device_ids=true | all-gather | bytes 81920 | tf_op jit(solution)/shard_map/all_gather | solution.py:84
  218.5 5.6 %all_gather.28 = f32[64,2,128]{0,1,2:T(2,128)S(1)} all-gather(f32[64,2,32]{0,1,2:T(2,128)S(1)} %multiply_add_fusion.2), channel_id=1, replica_groups=mesh['chan'=2,'srow'=4,'scol'=4] {'srow'}, dimensions={2}, use_global_device_ids=true | all-gather | bytes 81920 | tf_op jit(solution)/shard_map/all_gather | solution.py:62
  224.7 6.2 %subtract_reduce_fusion.3 = (f32[128,128]{1,0:T(8,128)S(1)}, f32[128,128]{1,0:T(8,128)S(1)}) fusion(f32[64,128]{1,0:T(8,128)S(1)} %copy.144, f32[64,128]{1,0:T(8,128)S(1)} %copy.143, f32[64,128]{1,0:T(8,128)S(1)} %copy.142, f32[64,128]{1,0:T(8,128)S(1)} %copy.141, bf16[64,2,128,128]{3,2,1,0:T(8,128)(2,1)} %bitcast.197), kind=kLoop, calls=%fused_computation.33 | loop fusion | flops 16744448 | bytes 4456448 | tf_op jit(solution)/shard_map/reduce_sum | solution.py:31
  231.5 4.1 add_reduce_fusion.2
  236.4 38.9 %psum.37 = f32[]{:T(128)} all-reduce(f32[]{:T(128)} %get-tuple-element.39), channel_id=1, replica_groups=mesh['chan'=2,'srow'=4,'scol'=4] {'chan','srow','scol'}, use_global_device_ids=true, to_apply=%region_27.28 | all-reduce | flops 1 | bytes 8 | tf_op jit(solution)/shard_map/psum | solution.py:64
  276.0 0.8 copy.147
  277.6 33.9 %all-reduce.13.cloned.1.call-done = f32[64,2,128]{0,1,2:T(2,128)} async-done(((f32[64,2,128]{0,1,2:T(2,128)}), f32[64,2,128]{0,1,2:T(2,128)}) %all-reduce.13.cloned.1.call-update) | async-done | bytes 65552
  311.5 0.8 multiply_add_fusion.1
  312.3 13.6 %all_gather.31 = f32[64,2,128]{0,1,2:T(2,128)S(1)} all-gather(f32[64,2,32]{0,1,2:T(2,128)S(1)} %multiply_add_fusion.1), channel_id=1, replica_groups=mesh['chan'=2,'srow'=4,'scol'=4] {'scol'}, dimensions={2}, use_global_device_ids=true | all-gather | bytes 81920 | tf_op jit(solution)/shard_map/all_gather | solution.py:84
  325.9 5.4 %all_gather.30 = f32[64,2,128]{0,1,2:T(2,128)S(1)} all-gather(f32[64,2,32]{0,1,2:T(2,128)S(1)} %multiply_add_fusion.1), channel_id=1, replica_groups=mesh['chan'=2,'srow'=4,'scol'=4] {'srow'}, dimensions={2}, use_global_device_ids=true | all-gather | bytes 81920 | tf_op jit(solution)/shard_map/all_gather | solution.py:62
  331.8 6.2 %subtract_reduce_fusion.1 = (f32[128,128]{1,0:T(8,128)S(1)}, f32[128,128]{1,0:T(8,128)S(1)}) fusion(f32[64,128]{1,0:T(8,128)S(1)} %copy.152, f32[64,128]{1,0:T(8,128)S(1)} %copy.151, f32[64,128]{1,0:T(8,128)S(1)} %copy.150, f32[64,128]{1,0:T(8,128)S(1)} %copy.149, bf16[64,2,128,128]{3,2,1,0:T(8,128)(2,1)} %bitcast.198), kind=kLoop, calls=%fused_computation.28 | loop fusion | flops 16744448 | bytes 4456448 | tf_op jit(solution)/shard_map/reduce_sum | solution.py:31
  338.6 4.1 add_reduce_fusion
  343.6 38.9 %psum.38 = f32[]{:T(128)} all-reduce(f32[]{:T(128)} %get-tuple-element.36), channel_id=1, replica_groups=mesh['chan'=2,'srow'=4,'scol'=4] {'chan','srow','scol'}, use_global_device_ids=true, to_apply=%region_36.37 | all-reduce | flops 1 | bytes 8 | tf_op jit(solution)/shard_map/psum | solution.py:64
  384.7 33.9 %all-reduce.15.cloned.1.call-done = f32[64,2,128]{0,1,2:T(2,128)} async-done(((f32[64,2,128]{0,1,2:T(2,128)}), f32[64,2,128]{0,1,2:T(2,128)}) %all-reduce.15.cloned.1.call-update) | async-done | bytes 65552
  418.6 0.8 fusion.21
  420.1 8.3 %psum.39 = f32[64,1,2,32]{0,2,3,1:T(2,128)S(1)} all-reduce(f32[64,1,2,32]{0,2,3,1:T(2,128)S(1)} %get-tuple-element.34), channel_id=1, replica_groups=mesh['chan'=2,'srow'=4,'scol'=4] {'chan'}, use_global_device_ids=true, to_apply=%region_37.38 | all-reduce | flops 4096 | bytes 32768 | tf_op jit(solution)/shard_map/psum | solution.py:94
  (100 shorter events, 15.8 us)
Async XLA Ops:
  7.2 28.6 %copy-start.4 = (bf16[1,2,128,128]{3,2,1,0:T(8,128)(2,1)S(1)}, bf16[1,2,128,128]{3,2,1,0:T(8,128)(2,1)}, u32[]{:S(2)}) copy-start(bf16[1,2,128,128]{3,2,1,0:T(8,128)(2,1)} %param.8) | copy-start | bytes 196612
  7.2 80.0 %reduce-scatter.5.cloned.1.call-start = ((), (), s32[]{:S(2)}) async-start(), calls=%async_computation.4 | async-start | bytes 81920 | tf_op jit(solution)/shard_map/reduce_scatter | solution.py:89
  29.5 6.9 %copy-start = (bf16[1,64,2,128,128]{4,3,2,1,0:T(8,128)(2,1)S(1)}, bf16[1,64,2,128,128]{4,3,2,1,0:T(8,128)(2,1)}, u32[]{:S(2)}) copy-start(bf16[1,64,2,128,128]{4,3,2,1,0:T(8,128)(2,1)} %param.9) | copy-start | bytes 12582916
  29.5 13.3 %copy-start.10 = (u32[32]{0:T(128)S(1)}, u32[32]{0:T(128)}, u32[]{:S(2)}) copy-start(u32[32]{0:T(128)} %constant.53) | copy-start | bytes 388
  29.5 56.8 %copy-start.8 = (f32[8]{0:T(128)S(1)}, f32[8]{0:T(128)}, u32[]{:S(2)}) copy-start(f32[8]{0:T(128)} %param.14) | copy-start | bytes 100
  29.5 56.8 %copy-start.9 = (s32[64]{0:T(128)S(1)}, s32[64]{0:T(128)}, u32[]{:S(2)}) copy-start(s32[64]{0:T(128)} %param.15) | copy-start | bytes 772
  29.6 67.4 %copy-start.5 = (f32[1,64,2,32]{1,3,2,0:T(8,128)S(1)}, f32[1,64,2,32]{1,3,2,0:T(8,128)}, u32[]{:S(2)}) copy-start(f32[1,64,2,32]{1,3,2,0:T(8,128)} %param.11) | copy-start | bytes 49156
  29.6 67.4 %copy-start.6 = (f32[1,64,2,32]{1,3,2,0:T(8,128)S(1)}, f32[1,64,2,32]{1,3,2,0:T(8,128)}, u32[]{:S(2)}) copy-start(f32[1,64,2,32]{1,3,2,0:T(8,128)} %param.13) | copy-start | bytes 49156
  29.6 67.3 %copy-start.7 = (f32[64,1,2,32]{0,3,2,1:T(8,128)S(1)}, f32[64,1,2,32]{0,3,2,1:T(8,128)}, u32[]{:S(2)}) copy-start(f32[64,1,2,32]{0,3,2,1:T(8,128)} %param.12) | copy-start | bytes 49156
  41.3 55.6 %all-reduce.9.cloned.1.call-start = ((), (), s32[]{:S(2)}) async-start(), calls=%async_computation.8 | async-start | bytes 262144
  42.1 127.4 %reduce-scatter.7.cloned.1.call-start = ((), (), s32[]{:S(2)}) async-start(), calls=%async_computation.5 | async-start | bytes 81920 | tf_op jit(solution)/shard_map/reduce_scatter | solution.py:89
  117.3 6.8 %copy-start.1 = (bf16[1,64,2,128,128]{4,3,2,1,0:T(8,128)(2,1)S(1)}, bf16[1,64,2,128,128]{4,3,2,1,0:T(8,128)(2,1)}, u32[]{:S(2)}) copy-start(bf16[1,64,2,128,128]{4,3,2,1,0:T(8,128)(2,1)} %param.9) | copy-start | bytes 12582916
  129.0 75.2 %all-reduce.11.cloned.1.call-start = ((), (), s32[]{:S(2)}) async-start(), calls=%async_computation.9 | async-start | bytes 262144
  169.5 107.4 %reduce-scatter.9.cloned.1.call-start = ((), (), s32[]{:S(2)}) async-start(), calls=%async_computation.6 | async-start | bytes 81920 | tf_op jit(solution)/shard_map/reduce_scatter | solution.py:89
  224.6 6.8 %copy-start.2 = (bf16[1,64,2,128,128]{4,3,2,1,0:T(8,128)(2,1)S(1)}, bf16[1,64,2,128,128]{4,3,2,1,0:T(8,128)(2,1)}, u32[]{:S(2)}) copy-start(bf16[1,64,2,128,128]{4,3,2,1,0:T(8,128)(2,1)} %param.9) | copy-start | bytes 12582916
  236.4 75.1 %all-reduce.13.cloned.1.call-start = ((), (), s32[]{:S(2)}) async-start(), calls=%async_computation.10 | async-start | bytes 262144
  276.8 107.2 %reduce-scatter.11.cloned.1.call-start = ((), (), s32[]{:S(2)}) async-start(), calls=%async_computation.7 | async-start | bytes 81920 | tf_op jit(solution)/shard_map/reduce_scatter | solution.py:89
  331.8 6.8 %copy-start.3 = (bf16[1,64,2,128,128]{4,3,2,1,0:T(8,128)(2,1)S(1)}, bf16[1,64,2,128,128]{4,3,2,1,0:T(8,128)(2,1)}, u32[]{:S(2)}) copy-start(bf16[1,64,2,128,128]{4,3,2,1,0:T(8,128)(2,1)} %param.9) | copy-start | bytes 12582916
  343.5 75.1 %all-reduce.15.cloned.1.call-start = ((), (), s32[]{:S(2)}) async-start(), calls=%async_computation.11 | async-start | bytes 262144
Sparse Core Ops, SparseCore 0:
  41.4 20.3 reduce-scatter.4
  64.2 32.6 all-reduce.8
  129.1 18.5 reduce-scatter.6
  169.6 34.5 all-reduce.10
  236.5 18.5 reduce-scatter.8
  276.9 34.5 all-reduce.12
  343.6 18.5 reduce-scatter.10
  384.1 34.5 all-reduce.14
where the time goes:
time: 438 us; the launch traced here: 437 us
  blocking collectives  244 us (56%)
  waiting for transfers between devices  111 us (25%)
  other arithmetic  51.5 us (12%)
  between operations  19.1 us (4%)
  local copies, waits for them, and re-layouts  10.6 us (2%)
    psum x4, blocking collectives, sweep_terms(): total = lax.psum(power, ('chan', 'srow', 'scol'))  158 us
    unnamed x12, waiting for transfers between devices  111 us
    all_gather x4, blocking collectives, shards(): g_row = lax.all_gather(g, 'scol', axis=2, tiled=True)  55.9 us
    reduce_sum x4, other arithmetic, local_terms(): pred_real = jnp.sum(r_real * z_real - r_imag * z_imag, axis=0)  24.7 us
    all_gather x4, blocking collectives, sweep_terms(): g_col = lax.all_gather(own_gains, 'srow', axis=2, tiled=True)  22 us
    reduce_sum x4, other arithmetic, local_terms(): cross_real = jnp.sum(z_real * w_real[None] + z_imag * w_imag[None], axis=-1)  16.5 us
  transfers between devices with their start and end apart: 8, of which 4 were waited for; matrix products, arithmetic and copies ran while one was open for 2% of the time, Pallas kernels for 0%

commit v1 on v0

--- a/solution.py
+++ b/solution.py
@@ -9,6 +9,7 @@
 ITERS = 4
 EPS = 1e-05
 STEP = 0.5
+follow_samples_all = lambda chunk: lax.psum(lax.psum(chunk, axis_name=("srow", "scol")), "chan")
 
 
 def basis_table(groups, order):
@@ -61,7 +62,7 @@
 def sweep_terms(vis_block, model_block, weight, g_row, own_gains, rho_dir, groups):
     g_col = lax.all_gather(own_gains, "srow", axis=2, tiled=True)
     power, a_term, cross = local_terms(vis_block, model_block, weight, g_row, g_col)
-    total = lax.psum(power, ("chan", "srow", "scol"))
+    total = follow_samples_all(power)
     rho_eff = rho_dir * (total / (groups * STATIONS * STATIONS) + EPS)
     return (a_term, cross, rho_eff)
 

time: 438 us -> 466 us (1.064)
  waiting for transfers between devices: 111 us -> 140 us
    reduce_scatter x4, waiting for transfers between devices: 0.08 us -> 27.9 us  [shards(): lax.psum_scatter(a_term[:, None, :], 'scol', scatter_dimension=2, tiled=T...]
    psum x4 -> x8, blocking collectives: 158 us -> 156 us  [the longest x4 134 us: lax.psum(chunk, axis_name=('srow', 'scol'))]
  transfers between devices with their start and end apart: 8 -> 8, of which waited for: 4 -> 7; matrix products, arithmetic and copies ran while one was open for 2% -> 2% of each run, Pallas kernels for 0% -> 0%
where the time goes in v1:
time: 466 us; the launch traced here: 464 us
  blocking collectives  242 us (52%)
  waiting for transfers between devices  140 us (30%)
  other arithmetic  51.4 us (11%)
  between operations  19.1 us (4%)
  local copies, waits for them, and re-layouts  10.6 us (2%)
    psum x4, blocking collectives, lax.psum(chunk, axis_name=('srow', 'scol'))  134 us
    unnamed x12, waiting for transfers between devices  112 us
    all_gather x4, blocking collectives, shards(): g_row = lax.all_gather(g, 'scol', axis=2, tiled=True)  55.9 us
    reduce_scatter x4, waiting for transfers between devices, shards(): lax.psum_scatter(a_term[:, None, :], 'scol', scatter_dimension=2, tiled=T...  27.9 us
    reduce_sum x4, other arithmetic, local_terms(): pred_real = jnp.sum(r_real * z_real - r_imag * z_imag, axis=0)  24.7 us
    psum x4, blocking collectives, lax.psum(lax.psum(chunk, axis_name=('srow', 'scol')), 'chan')  22.3 us
    all_gather x4, blocking collectives, sweep_terms(): g_col = lax.all_gather(own_gains, 'srow', axis=2, tiled=True)  22 us
    reduce_sum x4, other arithmetic, local_terms(): cross_real = jnp.sum(z_real * w_real[None] + z_imag * w_imag[None], axis=-1)  16.5 us
  transfers between devices with their start and end apart: 8, of which 7 were waited for; matrix products, arithmetic and copies ran while one was open for 2% of the time, Pallas kernels for 0%

profile of v1, /device:TPU:0, one launch (start us, length us, event | category | flops | bytes accessed | tf_op | source)
XLA Modules:
  0.0 464.3 jit_solution(11140758476280336848)
XLA Ops:
  7.2 15.3 %all-gather.1 = f32[1,64,2,128]{1,3,2,0:T(8,128)S(1)} all-gather(f32[1,64,2,32]{1,3,2,0:T(8,128)} %param.11), channel_id=3, replica_groups=mesh['chan'=2,'srow'=4,'scol'=4] {'scol'}, dimensions={3}, use_global_device_ids=true | all-gather | bytes 81920 | tf_op jit(solution)/shard_map/all_gather | solution.py:85
  22.5 5.6 %all-gather = f32[1,64,2,128]{1,3,2,0:T(8,128)S(1)} all-gather(f32[1,64,2,32]{1,3,2,0:T(8,128)} %param.11), channel_id=2, replica_groups=mesh['chan'=2,'srow'=4,'scol'=4] {'srow'}, dimensions={3}, use_global_device_ids=true | all-gather | bytes 81920 | tf_op jit(solution)/shard_map/all_gather | solution.py:63
  29.6 6.2 %subtract_reduce_fusion.7 = (f32[128,128]{1,0:T(8,128)S(1)}, f32[128,128]{1,0:T(8,128)S(1)}) fusion(f32[64,128]{1,0:T(8,128)S(1)} %copy.125, f32[64,128]{1,0:T(8,128)S(1)} %copy.124, f32[64,128]{1,0:T(8,128)S(1)} %copy.122, f32[64,128]{1,0:T(8,128)S(1)} %copy.121, bf16[64,2,128,128]{3,2,1,0:T(8,128)(2,1)} %bitcast.195), kind=kLoop, calls=%fused_computation.43 | loop fusion | flops 16744448 | bytes 4456448 | tf_op jit(solution)/shard_map/reduce_sum | solution.py:32
  36.4 4.1 add_reduce_fusion.6
  42.8 34.9 %psum.63 = f32[]{:T(128)} all-reduce(f32[]{:T(128)} %get-tuple-element.47), channel_id=1, replica_groups=mesh['chan'=2,'srow'=4,'scol'=4] {'srow','scol'}, use_global_device_ids=true, to_apply=%region_9.10 | all-reduce | flops 1 | bytes 8 | tf_op jit(solution)/shard_map/psum | solution.py:12
  79.0 5.6 %psum.64 = f32[]{:T(128)} all-reduce(f32[]{:T(128)} %psum.63), channel_id=1, replica_groups=mesh['chan'=2,'srow'=4,'scol'=4] {'chan'}, use_global_device_ids=true, to_apply=%region_10.11 | all-reduce | flops 1 | bytes 8 | tf_op jit(solution)/shard_map/psum | solution.py:12
  87.4 9.6 %all-reduce.9.cloned.1.call-done = f32[64,2,128]{0,1,2:T(2,128)} async-done(((f32[64,2,128]{0,1,2:T(2,128)}), f32[64,2,128]{0,1,2:T(2,128)}) %all-reduce.9.cloned.1.call-update) | async-done | bytes 65552
  97.9 13.5 %all_gather.27 = f32[64,2,128]{0,1,2:T(2,128)S(1)} all-gather(f32[64,2,32]{0,1,2:T(2,128)S(1)} %get-tuple-element.45), channel_id=1, replica_groups=mesh['chan'=2,'srow'=4,'scol'=4] {'scol'}, dimensions={2}, use_global_device_ids=true | all-gather | bytes 81920 | tf_op jit(solution)/shard_map/all_gather | solution.py:85
  111.4 5.4 %all_gather.26 = f32[64,2,128]{0,1,2:T(2,128)S(1)} all-gather(f32[64,2,32]{0,1,2:T(2,128)S(1)} %get-tuple-element.45), channel_id=1, replica_groups=mesh['chan'=2,'srow'=4,'scol'=4] {'srow'}, dimensions={2}, use_global_device_ids=true | all-gather | bytes 81920 | tf_op jit(solution)/shard_map/all_gather | solution.py:63
  117.4 6.2 %subtract_reduce_fusion.5 = (f32[128,128]{1,0:T(8,128)S(1)}, f32[128,128]{1,0:T(8,128)S(1)}) fusion(f32[64,128]{1,0:T(8,128)S(1)} %copy.136, f32[64,128]{1,0:T(8,128)S(1)} %copy.135, f32[64,128]{1,0:T(8,128)S(1)} %copy.134, f32[64,128]{1,0:T(8,128)S(1)} %copy.133, bf16[64,2,128,128]{3,2,1,0:T(8,128)(2,1)} %bitcast.196), kind=kLoop, calls=%fused_computation.38 | loop fusion | flops 16744448 | bytes 4456448 | tf_op jit(solution)/shard_map/reduce_sum | solution.py:32
  124.2 4.1 add_reduce_fusion.4
  129.0 33.0 %psum.65 = f32[]{:T(128)} all-reduce(f32[]{:T(128)} %get-tuple-element.42), channel_id=1, replica_groups=mesh['chan'=2,'srow'=4,'scol'=4] {'srow','scol'}, use_global_device_ids=true, to_apply=%region_19.20 | all-reduce | flops 1 | bytes 8 | tf_op jit(solution)/shard_map/psum | solution.py:12
  162.1 5.6 %psum.66 = f32[]{:T(128)} all-reduce(f32[]{:T(128)} %psum.65), channel_id=1, replica_groups=mesh['chan'=2,'srow'=4,'scol'=4] {'chan'}, use_global_device_ids=true, to_apply=%region_20.21 | all-reduce | flops 1 | bytes 8 | tf_op jit(solution)/shard_map/psum | solution.py:12
  169.2 9.3 %reduce-scatter.7.cloned.1.call-done = f32[64,1,32]{0,1,2:T(1,128)} async-done(((f32[64,1,128]{0,1,2:T(1,128)}), f32[64,1,32]{0,1,2:T(1,128)}) %reduce-scatter.7.cloned.1.call-update) | async-done | bytes 8208 | tf_op jit(solution)/shard_map/reduce_scatter | solution.py:90
  179.2 34.2 %all-reduce.11.cloned.1.call-done = f32[64,2,128]{0,1,2:T(2,128)} async-done(((f32[64,2,128]{0,1,2:T(2,128)}), f32[64,2,128]{0,1,2:T(2,128)}) %all-reduce.11.cloned.1.call-update) | async-done | bytes 65552
  214.2 13.5 %all_gather.29 = f32[64,2,128]{0,1,2:T(2,128)S(1)} all-gather(f32[64,2,32]{0,1,2:T(2,128)S(1)} %multiply_add_fusion.2), channel_id=1, replica_groups=mesh['chan'=2,'srow'=4,'scol'=4] {'scol'}, dimensions={2}, use_global_device_ids=true | all-gather | bytes 81920 | tf_op jit(solution)/shard_map/all_gather | solution.py:85
  227.8 5.4 %all_gather.28 = f32[64,2,128]{0,1,2:T(2,128)S(1)} all-gather(f32[64,2,32]{0,1,2:T(2,128)S(1)} %multiply_add_fusion.2), channel_id=1, replica_groups=mesh['chan'=2,'srow'=4,'scol'=4] {'srow'}, dimensions={2}, use_global_device_ids=true | all-gather | bytes 81920 | tf_op jit(solution)/shard_map/all_gather | solution.py:63
  233.7 6.2 %subtract_reduce_fusion.3 = (f32[128,128]{1,0:T(8,128)S(1)}, f32[128,128]{1,0:T(8,128)S(1)}) fusion(f32[64,128]{1,0:T(8,128)S(1)} %copy.144, f32[64,128]{1,0:T(8,128)S(1)} %copy.143, f32[64,128]{1,0:T(8,128)S(1)} %copy.142, f32[64,128]{1,0:T(8,128)S(1)} %copy.141, bf16[64,2,128,128]{3,2,1,0:T(8,128)(2,1)} %bitcast.197), kind=kLoop, calls=%fused_computation.33 | loop fusion | flops 16744448 | bytes 4456448 | tf_op jit(solution)/shard_map/reduce_sum | solution.py:32
  240.5 4.1 add_reduce_fusion.2
  245.4 33.0 %psum.67 = f32[]{:T(128)} all-reduce(f32[]{:T(128)} %get-tuple-element.39), channel_id=1, replica_groups=mesh['chan'=2,'srow'=4,'scol'=4] {'srow','scol'}, use_global_device_ids=true, to_apply=%region_29.30 | all-reduce | flops 1 | bytes 8 | tf_op jit(solution)/shard_map/psum | solution.py:12
  278.5 5.6 %psum.68 = f32[]{:T(128)} all-reduce(f32[]{:T(128)} %psum.67), channel_id=1, replica_groups=mesh['chan'=2,'srow'=4,'scol'=4] {'chan'}, use_global_device_ids=true, to_apply=%region_30.31 | all-reduce | flops 1 | bytes 8 | tf_op jit(solution)/shard_map/psum | solution.py:12
  285.6 9.3 %reduce-scatter.9.cloned.1.call-done = f32[64,1,32]{0,1,2:T(1,128)} async-done(((f32[64,1,128]{0,1,2:T(1,128)}), f32[64,1,32]{0,1,2:T(1,128)}) %reduce-scatter.9.cloned.1.call-update) | async-done | bytes 8208 | tf_op jit(solution)/shard_map/reduce_scatter | solution.py:90
  295.6 34.2 %all-reduce.13.cloned.1.call-done = f32[64,2,128]{0,1,2:T(2,128)} async-done(((f32[64,2,128]{0,1,2:T(2,128)}), f32[64,2,128]{0,1,2:T(2,128)}) %all-reduce.13.cloned.1.call-update) | async-done | bytes 65552
  330.6 13.5 %all_gather.31 = f32[64,2,128]{0,1,2:T(2,128)S(1)} all-gather(f32[64,2,32]{0,1,2:T(2,128)S(1)} %multiply_add_fusion.1), channel_id=1, replica_groups=mesh['chan'=2,'srow'=4,'scol'=4] {'scol'}, dimensions={2}, use_global_device_ids=true | all-gather | bytes 81920 | tf_op jit(solution)/shard_map/all_gather | solution.py:85
  344.1 5.6 %all_gather.30 = f32[64,2,128]{0,1,2:T(2,128)S(1)} all-gather(f32[64,2,32]{0,1,2:T(2,128)S(1)} %multiply_add_fusion.1), channel_id=1, replica_groups=mesh['chan'=2,'srow'=4,'scol'=4] {'srow'}, dimensions={2}, use_global_device_ids=true | all-gather | bytes 81920 | tf_op jit(solution)/shard_map/all_gather | solution.py:63
  350.3 6.2 %subtract_reduce_fusion.1 = (f32[128,128]{1,0:T(8,128)S(1)}, f32[128,128]{1,0:T(8,128)S(1)}) fusion(f32[64,128]{1,0:T(8,128)S(1)} %copy.152, f32[64,128]{1,0:T(8,128)S(1)} %copy.151, f32[64,128]{1,0:T(8,128)S(1)} %copy.150, f32[64,128]{1,0:T(8,128)S(1)} %copy.149, bf16[64,2,128,128]{3,2,1,0:T(8,128)(2,1)} %bitcast.198), kind=kLoop, calls=%fused_computation.28 | loop fusion | flops 16744448 | bytes 4456448 | tf_op jit(solution)/shard_map/reduce_sum | solution.py:32
  357.1 4.1 add_reduce_fusion
  361.9 33.0 %psum.69 = f32[]{:T(128)} all-reduce(f32[]{:T(128)} %get-tuple-element.36), channel_id=1, replica_groups=mesh['chan'=2,'srow'=4,'scol'=4] {'srow','scol'}, use_global_device_ids=true, to_apply=%region_39.40 | all-reduce | flops 1 | bytes 8 | tf_op jit(solution)/shard_map/psum | solution.py:12
  395.0 5.6 %psum.70 = f32[]{:T(128)} all-reduce(f32[]{:T(128)} %psum.69), channel_id=1, replica_groups=mesh['chan'=2,'srow'=4,'scol'=4] {'chan'}, use_global_device_ids=true, to_apply=%region_40.41 | all-reduce | flops 1 | bytes 8 | tf_op jit(solution)/shard_map/psum | solution.py:12
  402.1 9.3 %reduce-scatter.11.cloned.1.call-done = f32[64,1,32]{0,1,2:T(1,128)} async-done(((f32[64,1,128]{0,1,2:T(1,128)}), f32[64,1,32]{0,1,2:T(1,128)}) %reduce-scatter.11.cloned.1.call-update) | async-done | bytes 8208 | tf_op jit(solution)/shard_map/reduce_scatter | solution.py:90
  412.1 34.3 %all-reduce.15.cloned.1.call-done = f32[64,2,128]{0,1,2:T(2,128)} async-done(((f32[64,2,128]{0,1,2:T(2,128)}), f32[64,2,128]{0,1,2:T(2,128)}) %all-reduce.15.cloned.1.call-update) | async-done | bytes 65552
  447.9 8.3 %psum.71 = f32[64,1,2,32]{0,2,3,1:T(2,128)S(1)} all-reduce(f32[64,1,2,32]{0,2,3,1:T(2,128)S(1)} %get-tuple-element.34), channel_id=1, replica_groups=mesh['chan'=2,'srow'=4,'scol'=4] {'chan'}, use_global_device_ids=true, to_apply=%region_41.42 | all-reduce | flops 4096 | bytes 32768 | tf_op jit(solution)/shard_map/psum | solution.py:95
  (104 shorter events, 21.3 us)
Async XLA Ops:
  7.2 28.6 %copy-start.4 = (bf16[1,2,128,128]{3,2,1,0:T(8,128)(2,1)S(1)}, bf16[1,2,128,128]{3,2,1,0:T(8,128)(2,1)}, u32[]{:S(2)}) copy-start(bf16[1,2,128,128]{3,2,1,0:T(8,128)(2,1)} %param.8) | copy-start | bytes 196612
  7.2 79.5 %reduce-scatter.5.cloned.1.call-start = ((), (), s32[]{:S(2)}) async-start(), calls=%async_computation.4 | async-start | bytes 81920 | tf_op jit(solution)/shard_map/reduce_scatter | solution.py:90
  29.5 6.9 %copy-start = (bf16[1,64,2,128,128]{4,3,2,1,0:T(8,128)(2,1)S(1)}, bf16[1,64,2,128,128]{4,3,2,1,0:T(8,128)(2,1)}, u32[]{:S(2)}) copy-start(bf16[1,64,2,128,128]{4,3,2,1,0:T(8,128)(2,1)} %param.9) | copy-start | bytes 12582916
  29.5 48.2 %copy-start.10 = (u32[32]{0:T(128)S(1)}, u32[32]{0:T(128)}, u32[]{:S(2)}) copy-start(u32[32]{0:T(128)} %constant.53) | copy-start | bytes 388
  29.5 56.4 %copy-start.8 = (f32[8]{0:T(128)S(1)}, f32[8]{0:T(128)}, u32[]{:S(2)}) copy-start(f32[8]{0:T(128)} %param.14) | copy-start | bytes 100
  29.5 56.4 %copy-start.9 = (s32[64]{0:T(128)S(1)}, s32[64]{0:T(128)}, u32[]{:S(2)}) copy-start(s32[64]{0:T(128)} %param.15) | copy-start | bytes 772
  29.6 67.4 %copy-start.5 = (f32[1,64,2,32]{1,3,2,0:T(8,128)S(1)}, f32[1,64,2,32]{1,3,2,0:T(8,128)}, u32[]{:S(2)}) copy-start(f32[1,64,2,32]{1,3,2,0:T(8,128)} %param.11) | copy-start | bytes 49156
  29.6 67.4 %copy-start.6 = (f32[1,64,2,32]{1,3,2,0:T(8,128)S(1)}, f32[1,64,2,32]{1,3,2,0:T(8,128)}, u32[]{:S(2)}) copy-start(f32[1,64,2,32]{1,3,2,0:T(8,128)} %param.13) | copy-start | bytes 49156
  29.6 67.4 %copy-start.7 = (f32[64,1,2,32]{0,3,2,1:T(8,128)S(1)}, f32[64,1,2,32]{0,3,2,1:T(8,128)}, u32[]{:S(2)}) copy-start(f32[64,1,2,32]{0,3,2,1:T(8,128)} %param.12) | copy-start | bytes 49156
  41.3 55.7 %all-reduce.9.cloned.1.call-start = ((), (), s32[]{:S(2)}) async-start(), calls=%async_computation.8 | async-start | bytes 262144
  42.1 136.4 %reduce-scatter.7.cloned.1.call-start = ((), (), s32[]{:S(2)}) async-start(), calls=%async_computation.5 | async-start | bytes 81920 | tf_op jit(solution)/shard_map/reduce_scatter | solution.py:90
  117.3 6.8 %copy-start.1 = (bf16[1,64,2,128,128]{4,3,2,1,0:T(8,128)(2,1)S(1)}, bf16[1,64,2,128,128]{4,3,2,1,0:T(8,128)(2,1)}, u32[]{:S(2)}) copy-start(bf16[1,64,2,128,128]{4,3,2,1,0:T(8,128)(2,1)} %param.9) | copy-start | bytes 12582916
  162.1 51.3 %all-reduce.11.cloned.1.call-start = ((), (), s32[]{:S(2)}) async-start(), calls=%async_computation.9 | async-start | bytes 262144
  169.2 125.7 %reduce-scatter.9.cloned.1.call-start = ((), (), s32[]{:S(2)}) async-start(), calls=%async_computation.6 | async-start | bytes 81920 | tf_op jit(solution)/shard_map/reduce_scatter | solution.py:90
  233.7 6.8 %copy-start.2 = (bf16[1,64,2,128,128]{4,3,2,1,0:T(8,128)(2,1)S(1)}, bf16[1,64,2,128,128]{4,3,2,1,0:T(8,128)(2,1)}, u32[]{:S(2)}) copy-start(bf16[1,64,2,128,128]{4,3,2,1,0:T(8,128)(2,1)} %param.9) | copy-start | bytes 12582916
  278.4 51.3 %all-reduce.13.cloned.1.call-start = ((), (), s32[]{:S(2)}) async-start(), calls=%async_computation.10 | async-start | bytes 262144
  285.5 125.9 %reduce-scatter.11.cloned.1.call-start = ((), (), s32[]{:S(2)}) async-start(), calls=%async_computation.7 | async-start | bytes 81920 | tf_op jit(solution)/shard_map/reduce_scatter | solution.py:90
  350.3 6.8 %copy-start.3 = (bf16[1,64,2,128,128]{4,3,2,1,0:T(8,128)(2,1)S(1)}, bf16[1,64,2,128,128]{4,3,2,1,0:T(8,128)(2,1)}, u32[]{:S(2)}) copy-start(bf16[1,64,2,128,128]{4,3,2,1,0:T(8,128)(2,1)} %param.9) | copy-start | bytes 12582916
  395.0 51.5 %all-reduce.15.cloned.1.call-start = ((), (), s32[]{:S(2)}) async-start(), calls=%async_computation.11 | async-start | bytes 262144
Sparse Core Ops, SparseCore 0:
  41.4 20.3 reduce-scatter.4
  64.2 32.7 all-reduce.8
  162.2 16.2 reduce-scatter.6
  180.8 32.5 all-reduce.10
  278.6 16.2 reduce-scatter.8
  297.1 32.5 all-reduce.12
  395.1 16.2 reduce-scatter.10
  413.8 32.5 all-reduce.14
